TPU v7x, 32 devices: a whole 2x2x4 slice. The times are simulated.
32 devices in a mesh: dp: 16 (over z, x, core), tensor: 2 (over y).
Axes of the slice: x: 2, y: 2, z: 4, core: 2. Of those that a mesh axis runs over, the one named last changes fastest.
Arguments:
- tokens: bfloat16 [16384, 768], P('dp'), may hold values from -6 to 6
- memory: bfloat16 [128, 256, 768], P('dp'), may hold values from -6 to 6
- groups: int32 [256], P('dp'), may hold values from 0 to 127, as said below
- norm_gains: float32 [3, 768], replicated, may hold values from 0.1 to 1.9
- norm_biases: float32 [3, 768], replicated, may hold values from -1.2 to 1.2
- self_qkv: bfloat16 [3, 768, 768], P(None, None, 'tensor'), may hold values from -0.3125 to 0.3125
- self_out: bfloat16 [768, 768], P('tensor'), may hold values from -0.625 to 0.625
- cross_query: bfloat16 [768, 768], P(None, 'tensor'), may hold values from -0.3125 to 0.3125
- cross_kv: bfloat16 [2, 768, 768], P(None, None, 'tensor'), may hold values from -0.3125 to 0.3125
- cross_out: bfloat16 [768, 768], P('tensor'), may hold values from -0.875 to 0.875
- mlp_up: bfloat16 [768, 3072], P(None, 'tensor'), may hold values from -0.21875 to 0.21875
- mlp_down: bfloat16 [3072, 768], P('tensor'), may hold values from -0.15625 to 0.15625
- cotangent: bfloat16 [16384, 768], P('dp'), may hold values from -6 to 6
Outputs:
- output: bfloat16 [16384, 768], P('dp')
- input_grad: bfloat16 [16384, 768], P('dp')
- memory_grad: bfloat16 [128, 256, 768], P('dp', None, 'tensor')
- norm_gains_grad: float32 [3, 768], replicated
- norm_biases_grad: float32 [3, 768], replicated
- self_qkv_grad: float32 [3, 768, 768], P(None, None, 'tensor')
- self_out_grad: float32 [768, 768], P('tensor')
- cross_query_grad: float32 [768, 768], P(None, 'tensor')
- cross_kv_grad: float32 [2, 768, 768], P(None, None, 'tensor')
- cross_out_grad: float32 [768, 768], P('tensor')
- mlp_up_grad: float32 [768, 3072], P(None, 'tensor')
- mlp_down_grad: float32 [3072, 768], P('tensor')
Inputs may be any that keep to these rules, and one draw needn't show every extreme that they name: `groups`: captions of index p of dp read only that index's images, numbers p * 8 to (p + 1) * 8 - 1, and each image is read by exactly two captions.
All inputs are finite; a program needn't handle non-finite values.
Results may differ from a plain program's by a relative error of at most 0.023.
The roundings to bfloat16 on the way count: a program that leaves them out, or rounds other values in their place, can miss the bound.
Values may be sent and summed in bfloat16 or wider, within the bound.
A program may use at most 192 MiB of HBM per device.

v0:
```python
import jax
import jax.numpy as jnp
from jax import lax
from jax.sharding import PartitionSpec as P

HEAD_DIM = 64


epsilon = 1e-05


def matmul(left_side, right_side):
    return jnp.dot(left_side, right_side, preferred_element_type=jnp.float32)


def outer_sum(left_side, right_side):
    return jnp.einsum("tf,td->fd", left_side, right_side, preferred_element_type=jnp.float32)


def back_product(grad_side, weight):
    return jnp.einsum("td,fd->tf", grad_side, weight, preferred_element_type=jnp.float32)


def exact_gelu(values):
    return jax.nn.gelu(values, approximate=False)


def normalize(values, gain_row, bias_row):
    average = jnp.mean(values, axis=-1, keepdims=True)
    centred = values - average
    inverse = lax.rsqrt(jnp.mean(centred * centred, axis=-1, keepdims=True) + epsilon)
    scaled = centred * inverse
    return (scaled * gain_row + bias_row, scaled, inverse)


def normalize_back(grad_out, scaled, inverse, gain_row):
    weighted = grad_out * gain_row
    result = inverse * (
        weighted
        - jnp.mean(weighted, axis=-1, keepdims=True)
        - scaled * jnp.mean(weighted * scaled, axis=-1, keepdims=True)
    )
    return (result, jnp.sum(grad_out * scaled, axis=0), jnp.sum(grad_out, axis=0))


def attention_scores(queries, key_heads, causal):
    scores = jnp.einsum(
        "clhe,ckhe->chlk", queries, key_heads, preferred_element_type=jnp.float32
    ) * HEAD_DIM ** (-0.5)
    if causal:
        allowed = lax.broadcasted_iota(jnp.int32, scores.shape, 2) >= lax.broadcasted_iota(
            jnp.int32, scores.shape, 3
        )
        scores = jnp.where(allowed, scores, -1e30)
    return scores


def attend_forward(queries, key_heads, value_heads, causal):
    scores = attention_scores(queries, key_heads, causal)
    row_top = jnp.max(scores, axis=-1, keepdims=True)
    log_total = row_top + jnp.log(jnp.sum(jnp.exp(scores - row_top), axis=-1, keepdims=True))
    weights = jnp.exp(scores - log_total).astype(jnp.bfloat16)
    mixed = jnp.einsum("chlk,ckhe->clhe", weights, value_heads, preferred_element_type=jnp.float32)
    return (mixed, log_total)


def attend_back(queries, key_heads, value_heads, log_total, grad_heads, causal):
    scores = attention_scores(queries, key_heads, causal)
    probs = jnp.exp(scores - log_total)
    probs_low = probs.astype(jnp.bfloat16)
    value_grad = jnp.einsum(
        "chlk,clhe->ckhe", probs_low, grad_heads, preferred_element_type=jnp.float32
    )
    prob_grad = jnp.einsum(
        "clhe,ckhe->chlk", grad_heads, value_heads, preferred_element_type=jnp.float32
    )
    score_grad = (probs * (prob_grad - jnp.sum(probs * prob_grad, axis=-1, keepdims=True))).astype(
        jnp.bfloat16
    )
    query_grad = jnp.einsum(
        "chlk,ckhe->clhe", score_grad, key_heads, preferred_element_type=jnp.float32
    ) * HEAD_DIM ** (-0.5)
    key_grad = jnp.einsum(
        "chlk,clhe->ckhe", score_grad, queries, preferred_element_type=jnp.float32
    ) * HEAD_DIM ** (-0.5)
    return (query_grad, key_grad, value_grad)


def shards(
    tokens,
    memory,
    groups,
    norm_gains,
    norm_biases,
    self_qkv,
    self_out,
    cross_query,
    cross_kv,
    cross_out,
    mlp_up,
    mlp_down,
    cotangent,
):
    captions = groups.shape[0]
    row_count = tokens.shape[0]
    length = row_count // captions
    model_width = tokens.shape[1]
    local_width = self_qkv.shape[2]
    local_heads = local_width // HEAD_DIM
    images = memory.shape[0]
    memory_span = memory.shape[1]
    heads_shape = (captions, length, local_heads, HEAD_DIM)
    inputs = tokens.astype(jnp.float32)
    first_norm, first_scaled, first_inverse = normalize(inputs, norm_gains[0], norm_biases[0])
    first_low = first_norm.astype(jnp.bfloat16)
    qkv_heads = jnp.einsum(
        "td,jdf->jtf", first_low, self_qkv, preferred_element_type=jnp.float32
    ).astype(jnp.bfloat16)
    queries = qkv_heads[0].reshape(heads_shape)
    key_heads = qkv_heads[1].reshape(heads_shape)
    value_heads = qkv_heads[2].reshape(heads_shape)
    mixed_heads, self_total = attend_forward(queries, key_heads, value_heads, True)
    mixed_low = mixed_heads.reshape(row_count, local_width).astype(jnp.bfloat16)
    hidden_one = inputs + lax.psum(matmul(mixed_low, self_out), "tensor")
    second, second_scaled, second_inverse = normalize(hidden_one, norm_gains[1], norm_biases[1])
    second_low = second.astype(jnp.bfloat16)
    local_groups = groups - lax.axis_index("dp") * images
    cross_queries = matmul(second_low, cross_query).astype(jnp.bfloat16).reshape(heads_shape)
    flat_memory = memory.reshape(images * memory_span, model_width)
    memory_kv = jnp.einsum(
        "md,jdf->jmf", flat_memory, cross_kv, preferred_element_type=jnp.float32
    ).astype(jnp.bfloat16)
    memory_kv = memory_kv.reshape(2, images, memory_span, local_width)
    caption_kv = jnp.take(memory_kv, local_groups, axis=1).reshape(
        2, captions, memory_span, local_heads, HEAD_DIM
    )
    cross_mixed, cross_total = attend_forward(cross_queries, caption_kv[0], caption_kv[1], False)
    cross_low = cross_mixed.reshape(row_count, local_width).astype(jnp.bfloat16)
    hidden_two = hidden_one + lax.psum(matmul(cross_low, cross_out), "tensor")
    third_norm, third_scaled, third_inverse = normalize(hidden_two, norm_gains[2], norm_biases[2])
    third_low = third_norm.astype(jnp.bfloat16)
    upward = matmul(third_low, mlp_up)
    active_low = exact_gelu(upward).astype(jnp.bfloat16)
    output = (
        hidden_two
        + lax.psum(matmul(active_low, mlp_down).astype(jnp.bfloat16), "tensor").astype(jnp.float32)
    ).astype(jnp.bfloat16)
    grad_output = cotangent.astype(jnp.float32)
    down_grad = outer_sum(active_low, cotangent)
    active_grad = back_product(cotangent, mlp_down)
    unused_value, gelu_back = jax.vjp(exact_gelu, upward)
    upward_grad = gelu_back(active_grad)[0].astype(jnp.bfloat16)
    up_grad = outer_sum(third_low, upward_grad)
    third_grad = lax.psum(back_product(upward_grad, mlp_up).astype(jnp.bfloat16), "tensor").astype(
        jnp.float32
    )
    back_three, gain_three, bias_three = normalize_back(
        third_grad, third_scaled, third_inverse, norm_gains[2]
    )
    grad_hidden_two = grad_output + back_three
    cross_branch = grad_hidden_two.astype(jnp.bfloat16)
    cross_out_grad = outer_sum(cross_low, cross_branch)
    pick_table = (
        local_groups[:, None] == lax.broadcasted_iota(jnp.int32, (captions, images), 1)
    ).astype(jnp.float32)
    cross_mixed_grad = (
        back_product(cross_branch, cross_out).astype(jnp.bfloat16).reshape(heads_shape)
    )
    cross_query_heads, caption_key_grad, caption_value_grad = attend_back(
        cross_queries, caption_kv[0], caption_kv[1], cross_total, cross_mixed_grad, False
    )
    caption_pairs = jnp.stack([caption_key_grad, caption_value_grad]).reshape(
        2, captions, memory_span, local_width
    )
    pair_grads = jnp.einsum(
        "ci,jcmf->jimf", pick_table, caption_pairs, precision=lax.Precision.HIGHEST
    )
    pair_low = pair_grads.astype(jnp.bfloat16).reshape(2, images * memory_span, local_width)
    cross_query_low = cross_query_heads.reshape(row_count, local_width).astype(jnp.bfloat16)
    cross_query_grad = outer_sum(second_low, cross_query_low)
    cross_kv_grad = jnp.einsum(
        "md,jmf->jdf", flat_memory, pair_low, preferred_element_type=jnp.float32
    )
    memory_term = jnp.einsum("jmf,jdf->md", pair_low, cross_kv, preferred_element_type=jnp.float32)
    memory_term = memory_term.reshape(images, memory_span, model_width)
    memory_grad = lax.psum_scatter(
        memory_term.astype(jnp.bfloat16), "tensor", scatter_dimension=2, tiled=True
    )
    second_grad = lax.psum(back_product(cross_query_low, cross_query), "tensor")
    back_two, gain_two, bias_two = normalize_back(
        second_grad, second_scaled, second_inverse, norm_gains[1]
    )
    grad_hidden_one = grad_hidden_two + back_two
    gains_later = jnp.stack([gain_two, gain_three])
    biases_later = jnp.stack([bias_two, bias_three])
    early_parts = (
        up_grad,
        down_grad,
        cross_query_grad,
        cross_kv_grad,
        cross_out_grad,
        gains_later,
        biases_later,
    )
    early_parts = lax.psum(
        (
            up_grad,
            down_grad,
            cross_query_grad,
            cross_kv_grad,
            cross_out_grad,
            gains_later,
            biases_later,
        ),
        "dp",
    )
    self_branch = grad_hidden_one.astype(jnp.bfloat16)
    self_out_grad = outer_sum(mixed_low, self_branch)
    mixed_grad = back_product(self_branch, self_out).astype(jnp.bfloat16).reshape(heads_shape)
    query_grad, key_grad, value_grad = attend_back(
        queries, key_heads, value_heads, self_total, mixed_grad, True
    )
    qkv_grad_low = (
        jnp.stack([query_grad, key_grad, value_grad])
        .astype(jnp.bfloat16)
        .reshape(3, row_count, local_width)
    )
    self_qkv_grad = jnp.einsum(
        "td,jtf->jdf", first_low, qkv_grad_low, preferred_element_type=jnp.float32
    )
    first_grad = lax.psum(
        jnp.einsum(
            "jtf,jdf->td", qkv_grad_low, self_qkv, preferred_element_type=jnp.float32
        ).astype(jnp.bfloat16),
        "tensor",
    ).astype(jnp.float32)
    back_one, gain_one, bias_one = normalize_back(
        first_grad, first_scaled, first_inverse, norm_gains[0]
    )
    input_grad = (grad_hidden_one + back_one).astype(jnp.bfloat16)
    qkv_total, self_out_total, gain_first, bias_first = lax.psum(
        (self_qkv_grad, self_out_grad, gain_one, bias_one), "dp"
    )
    (
        up_total,
        down_total,
        cross_query_total,
        cross_kv_total,
        cross_out_total,
        gains_total,
        biases_total,
    ) = early_parts
    norm_gains_grad = jnp.concatenate([gain_first[None], gains_total], axis=0)
    norm_biases_grad = jnp.concatenate([bias_first[None], biases_total], axis=0)
    return (
        output,
        input_grad,
        memory_grad,
        norm_gains_grad,
        norm_biases_grad,
        qkv_total,
        self_out_total,
        cross_query_total,
        cross_kv_total,
        cross_out_total,
        up_total,
        down_total,
    )


def solution(mesh):
    return jax.shard_map(
        shards,
        mesh=mesh,
        in_specs=(
            P("dp", None),
            P("dp", None, None),
            P("dp"),
            P(),
            P(),
            P(None, None, "tensor"),
            P("tensor", None),
            P(None, "tensor"),
            P(None, None, "tensor"),
            P("tensor", None),
            P(None, "tensor"),
            P("tensor", None),
            P("dp", None),
        ),
        out_specs=(
            P("dp", None),
            P("dp", None),
            P("dp", None, "tensor"),
            P(),
            P(),
            P(None, None, "tensor"),
            P("tensor", None),
            P(None, "tensor"),
            P(None, None, "tensor"),
            P("tensor", None),
            P(None, "tensor"),
            P("tensor", None),
        ),
        check_vma=False,
    )
```

profile of v0, /device:TPU:0, one launch (start us, length us, event | category | flops | bytes accessed | tf_op | source)
XLA Modules:
  0.0 970.7 jit_solution(12079640574562860956)
XLA Ops:
  49.6 6.6 fusion.41
  56.2 4.7 copy.156
  61.0 6.0 gather_fusion
  74.0 4.6 copy.109
  78.6 4.6 copy.111
  83.3 54.6 %all-reduce.10.cloned.1.call-done = f32[1024,768]{1,0:T(8,128)} async-done(((f32[1024,768]{1,0:T(8,128)}), f32[1024,768]{1,0:T(8,128)}) %all-reduce.10.cloned.1.call-update) | async-done | bytes 3145744 | tf_op jit(solution)/shard_map/psum | solution.py:124
  169.3 10.4 %all-reduce.14.cloned.1.call-start = ((), (), s32[]{:S(2)}) async-start(), calls=%async_computation.3 | async-start | bytes 3145728 | tf_op jit(solution)/shard_map/psum | solution.py:154
  179.7 75.5 %all-reduce.12.cloned.1.call-done = f32[1024,768]{1,0:T(8,128)} async-done(((f32[1024,768]{1,0:T(8,128)}), f32[1024,768]{1,0:T(8,128)}) %all-reduce.12.cloned.1.call-update) | async-done | bytes 3145744 | tf_op jit(solution)/shard_map/psum | solution.py:139
  264.1 18.0 %add_convert_fusion = (bf16[1024,1536]{1,0:T(8,128)(2,1)S(1)}, f32[1024,1536]{1,0:T(8,128)}) fusion(f32[1024,1536]{1,0:T(8,128)S(1)} %fusion.81, bf16[1024,768]{1,0:T(8,128)(2,1)S(1)} %copy-done.45, bf16[1536,768]{1,0:T(8,128)(2,1)S(1)} %copy-done), kind=kOutput, calls=%fused_computation.11 | convolution fusion | flops 2529165312 | bytes 19660800 | tf_op jit(solution)/shard_map/td,fd->tf/dot_general | solution.py:21
  287.7 51.6 %all-reduce.14.cloned.1.call-done = bf16[1024,768]{1,0:T(8,128)(2,1)} async-done(((bf16[1024,768]{1,0:T(8,128)(2,1)}), bf16[1024,768]{1,0:T(8,128)(2,1)}) %all-reduce.14.cloned.1.call-update) | async-done | bytes 1572880 | tf_op jit(solution)/shard_map/psum | solution.py:154
  339.3 4.3 fusion.33
  355.0 6.6 multiply_reduce_fusion
  361.6 4.5 multiply_convert_fusion
  375.8 4.1 fusion.90
  380.4 8.0 multiply_convert_fusion.1
  388.3 6.7 fusion.69
  395.1 6.7 copy.138
  401.8 6.0 broadcast_multiply_fusion
  407.7 6.8 copy.137
  414.5 7.9 convert_bitcast_fusion
  428.1 5.4 copy.160
  433.5 4.7 copy.177
  438.3 7.4 fusion.92
  449.5 4.6 fusion.80
  454.1 11.7 %all-reduce.16.cloned.1.call-done = f32[1024,768]{1,0:T(8,128)} async-done(((f32[1024,768]{1,0:T(8,128)}), f32[1024,768]{1,0:T(8,128)}) %all-reduce.16.cloned.1.call-update) | async-done | bytes 3145744 | tf_op jit(solution)/shard_map/psum | solution.py:189
  519.0 7.5 fusion.47
  534.0 4.1 convolution_bitcast_fusion
  544.8 60.1 %all-reduce.20.cloned.1.call-done = (bf16[1024,768]{1,0:T(8,128)(2,1)}, bf16[1024,768]{1,0:T(8,128)(2,1)}) async-done(((bf16[1024,768]{1,0:T(8,128)(2,1)}, bf16[1024,768]{1,0:T(8,128)(2,1)}), (bf16[1024,768]{1,0:T(8,128)(2,1)}, bf16[1024,768]{1,0:T(8,128)(2,1)})) %all-reduce.20.cloned.1.call-update) | async-done | bytes 3145744 | tf_op jit(solution)/shard_map/psum | solution.py:146
  607.8 65.0 %all-reduce = (f32[2,768]{1,0:T(2,128)S(1)}, f32[1,768]{1,0:T(1,128)S(1)}, f32[2,768]{1,0:T(2,128)S(1)}, f32[1,768]{1,0:T(1,128)S(1)}) all-reduce(f32[2,768]{1,0:T(2,128)S(1)} %pad_maximum_fusion.2, f32[1,768]{1,0:T(1,128)S(1)} %broadcast_in_dim.25, f32[2,768]{1,0:T(2,128)S(1)} %pad_maximum_fusion.3, ...), channel_id=1, replica_groups=mesh['dp'=16,'tensor'=2] {'dp'}, use_global_device_ids=true, to_apply=%region_29.30 | all-reduce | flops 4608 | bytes 36864 | tf_op jit(solution)/shard_map/psum | solution.py:205
  674.0 4.1 add_convert_fusion.1
  681.0 264.8 %all-reduce.18.cloned.1.call-done = (f32[3,768,384]{1,2,0:T(8,128)}, f32[384,768]{1,0:T(8,128)}, f32[768,384]{1,0:T(8,128)}, f32[2,768,384]{1,2,0:T(8,128)}, f32...) async-done(((f32[3,768,384]{1,2,0:T(8,128)}, f32[384,768]{1,0:T(8,128)}, f32[768,384]{1,0:T(8,128)}, f32[2,768,384]{1,2,0:T(8,128)}, f32[384,768]{1,0:T(8,128)}, ...) | async-done | bytes 18874384 | tf_op jit(solution)/shard_map/psum | solution.py:241
  945.9 5.3 copy.142
  (260 shorter events, 212.2 us)
Async XLA Ops:
  7.2 256.9 %copy-start = (bf16[1536,768]{1,0:T(8,128)(2,1)S(1)}, bf16[1536,768]{1,0:T(8,128)(2,1)}, u32[]{:S(2)}) copy-start(bf16[1536,768]{1,0:T(8,128)(2,1)} %param.24) | copy-start | bytes 7077892
  7.2 130.7 %all-reduce.10.cloned.1.call-start = ((), (), s32[]{:S(2)}) async-start(), calls=%async_computation.1 | async-start | bytes 6291456 | tf_op jit(solution)/shard_map/psum | solution.py:124
  9.1 6.1 copy-start.51
  49.3 205.9 %all-reduce.12.cloned.1.call-start = ((), (), s32[]{:S(2)}) async-start(), calls=%async_computation.2 | async-start | bytes 6291456 | tf_op jit(solution)/shard_map/psum | solution.py:139
  56.2 4.7 copy-start.63
  154.4 4.2 copy-start.19
  169.3 170.0 %all-reduce.14.cloned.1.call-start = ((), (), s32[]{:S(2)}) async-start(), calls=%async_computation.3 | async-start | bytes 3145728 | tf_op jit(solution)/shard_map/psum | solution.py:154
  258.4 5.6 copy-start.7
  264.1 18.0 %copy-start.30 = (f32[1024,1536]{1,0:T(8,128)}, f32[1024,1536]{1,0:T(8,128)S(1)}, u32[]{:S(2)}) copy-start(f32[1024,1536]{1,0:T(8,128)S(1)} %fusion.81) | copy-start | bytes 18874372
  287.6 178.2 %all-reduce.16.cloned.1.call-start = ((), (), s32[]{:S(2)}) async-start(), calls=%async_computation.4 | async-start | bytes 6291456 | tf_op jit(solution)/shard_map/psum | solution.py:189
  339.3 4.4 copy-start.8
  339.3 4.4 copy-start.31
  343.6 4.3 copy-start.38
  361.6 6.2 copy-start.18
  375.8 4.1 copy-start.35
  379.9 159.0 %reduce-scatter.4.cloned.1.call-start = ((), (), s32[]{:S(2)}) async-start(), calls=%async_computation.5 | async-start | bytes 4718592
  380.4 8.0 copy-start.21
  414.5 9.6 copy-start.66
  438.2 166.7 %all-reduce.20.cloned.1.call-start = ((), (), s32[]{:S(2)}) async-start(), calls=%async_computation.7 | async-start | bytes 6291456 | tf_op jit(solution)/shard_map/psum | solution.py:146
  438.3 7.4 copy-start.37
  465.8 4.7 copy-start.14
  470.5 4.5 copy-start.39
  476.1 5.4 copy-start.42
  518.7 7.8 copy-start.36
  518.7 427.1 %all-reduce.18.cloned.1.call-start = ((), (), s32[]{:S(2)}) async-start(), calls=%async_computation.6 | async-start | bytes 37748736 | tf_op jit(solution)/shard_map/psum | solution.py:241
  519.0 7.5 copy-start.44
  674.0 4.8 copy-start.29
  945.8 5.3 copy-start.40
  951.2 4.5 copy-start.47
  953.1 4.5 copy-start.32
  956.6 4.2 slice-start
  957.7 5.7 copy-start.1
  (46 other events, 122.6 us)
Sparse Core Ops, SparseCore 0:
  49.4 88.4 all-reduce.9
  169.4 85.7 all-reduce.11
  287.7 51.4 all-reduce.13
  380.0 85.7 all-reduce.15
  467.9 43.3 reduce-scatter.3
  518.8 85.9 all-reduce.19
  611.6 334.2 all-reduce.17
where the time goes:
time: 981 us; the launch traced here: 971 us
  waiting for transfers between devices  519 us (53%)
  local copies, waits for them, and re-layouts  164 us (17%)
  matrix products  141 us (14%)
  blocking collectives  65 us (7%)
  other arithmetic  55.3 us (6%)
  between operations  15.6 us (2%)
  starting transfers between devices  11.5 us (1%)
    psum x1, waiting for transfers between devices, shards(): lax.psum((self_qkv_grad, self_out_grad, gain_one, bias_one), 'dp')  265 us
    psum x1, waiting for transfers between devices, shards(): hidden_two = hidden_one + lax.psum(matmul(cross_low, cross_out), 'tensor')  75.5 us
    psum x1, blocking collectives, shards(): lax.psum((up_grad, down_grad, cross_query_grad, cross_kv_grad, cross_out_...  65 us
    psum x1, waiting for transfers between devices, shards(): lax.psum(matmul(active_low, mlp_down).astype(jnp.bfloat16), 'tensor')  60.1 us
    unnamed x155, local copies, waits for them, and re-layouts  57.6 us
    psum x1, waiting for transfers between devices, shards(): hidden_one = inputs + lax.psum(matmul(mixed_low, self_out), 'tensor')  54.6 us
    psum x1, waiting for transfers between devices, shards(): lax.psum(back_product(upward_grad, mlp_up).astype(jnp.bfloat16), 'tensor')  51.6 us
    dot_general x5, matrix products, back_product(): jnp.einsum('td,fd->tf', grad_side, weight, preferred_element_type=jnp.flo...  27.8 us
  transfers between devices with their start and end apart: 7, of which 6 were waited for; matrix products, arithmetic and copies ran while one was open for 19% of the time, Pallas kernels for 0%

commit v1 on v0

v1 whole, which is shorter than its diff:
```python
import functools

import jax
import jax.numpy as jnp
from jax import lax
from jax.experimental import pallas as pl
from jax.experimental.pallas import tpu as pltpu
from jax.sharding import PartitionSpec as P

HEAD_DIM = 64
SCALE = HEAD_DIM**-0.5
PAIR = 2 * HEAD_DIM
EPSILON = 1e-05
ROOT_HALF = 0.7071067811865476
PDF_SCALE = 0.3989422804014327
MESH = pl.DeviceIdType.MESH
LOW = jnp.bfloat16
F32 = jnp.float32
VMEM_LIMIT = 60 * 1024 * 1024
ANY = pl.BlockSpec(memory_space=pl.ANY)
VMEM = pl.BlockSpec(memory_space=pltpu.VMEM)


def nn(left, right):
    return lax.dot_general(left, right, (((1,), (0,)), ((), ())), preferred_element_type=F32)


def nt(left, right):
    return lax.dot_general(left, right, (((1,), (1,)), ((), ())), preferred_element_type=F32)


def tn(left, right):
    return lax.dot_general(left, right, (((0,), (0,)), ((), ())), preferred_element_type=F32)


def standardize(values):
    average = jnp.mean(values, axis=-1, keepdims=True)
    centred = values - average
    inverse = lax.rsqrt(jnp.mean(centred * centred, axis=-1, keepdims=True) + EPSILON)
    return centred * inverse, inverse


def standardize_back(grad_out, scaled, inverse, gain_row):
    weighted = grad_out * gain_row
    return inverse * (
        weighted
        - jnp.mean(weighted, axis=-1, keepdims=True)
        - scaled * jnp.mean(weighted * scaled, axis=-1, keepdims=True)
    )


def column_sum(values):
    return jnp.sum(values, axis=0, keepdims=True)


def softmax(scores):
    top = jnp.max(scores, axis=-1, keepdims=True)
    weights = jnp.exp(scores - top)
    return weights * (1.0 / jnp.sum(weights, axis=-1, keepdims=True))


def first_lanes():
    return lax.broadcasted_iota(jnp.int32, (1, PAIR), 1) < HEAD_DIM


def split_heads(values):
    zeros = jnp.zeros_like(values)
    first = first_lanes()
    return jnp.where(first, values, zeros), jnp.where(first, zeros, values)


def caption_mask(rows, length):
    query = lax.broadcasted_iota(jnp.int32, (rows, rows), 0)
    key = lax.broadcasted_iota(jnp.int32, (rows, rows), 1)
    return (query // length == key // length) & (query >= key)


def attend(queries, keys, values, allowed):
    mixed = []
    for part in split_heads(queries * jnp.asarray(SCALE, LOW)):
        scores = nt(part, keys)
        if allowed is not None:
            scores = jnp.where(allowed, scores, -1e30)
        mixed.append(nn(softmax(scores).astype(LOW), values))
    return jnp.where(first_lanes(), mixed[0], mixed[1]).astype(LOW)


def attend_back(queries, keys, values, grads, allowed):
    query_grads = []
    key_grad = None
    value_grad = None
    for part, grad in zip(split_heads(queries * jnp.asarray(SCALE, LOW)), split_heads(grads)):
        scores = nt(part, keys)
        if allowed is not None:
            scores = jnp.where(allowed, scores, -1e30)
        probs = softmax(scores)
        prob_grad = nt(grad, values)
        score_grad = probs * (prob_grad - jnp.sum(probs * prob_grad, axis=-1, keepdims=True))
        score_low = score_grad.astype(LOW)
        query_grads.append(nn(score_low, keys))
        more_keys = tn(score_low, part)
        more_values = tn(probs.astype(LOW), grad)
        key_grad = more_keys if key_grad is None else key_grad + more_keys
        value_grad = more_values if value_grad is None else value_grad + more_values
    query_grad = jnp.where(first_lanes(), query_grads[0], query_grads[1]) * SCALE
    return query_grad.astype(LOW), key_grad.astype(LOW), value_grad.astype(LOW)


class Stores:
    def __init__(self, sems):
        self.sems = sems
        self.copies = []

    def __call__(self, source, target):
        copy = pltpu.make_async_copy(source, target, self.sems.at[len(self.copies)])
        copy.start()
        self.copies.append(copy)

    def wait(self):
        for copy in self.copies:
            copy.wait()


def self_forward(length, x, gains, biases, qkv0, qkv1, out0, out1, h1, s0, s1, o0, o1):
    scaled, _ = standardize(x[...].astype(F32))
    low = (scaled * gains[0:1] + biases[0:1]).astype(LOW)
    pair_rows = 2 * length
    for weight, saved in ((qkv0, s0), (qkv1, s1)):
        for j in range(3):
            saved[j] = nn(low, weight[j]).astype(LOW)
    groups = x.shape[0] // pair_rows
    for saved, mixed in ((s0, o0), (s1, o1)):

        @pl.loop(0, groups)
        def _(step):
            rows = pl.ds(pl.multiple_of(step * pair_rows, pair_rows), pair_rows)
            allowed = caption_mask(pair_rows, length)
            for lane in range(0, saved.shape[2], PAIR):
                lanes = slice(lane, lane + PAIR)
                mixed[rows, lanes] = attend(
                    saved[0, rows, lanes], saved[1, rows, lanes], saved[2, rows, lanes], allowed
                )

    h1[...] = x[...].astype(F32) + (nn(o0[...], out0[...]) + nn(o1[...], out1[...]))


def cross_forward(span, h1, memory, gains, biases, q0, q1, kv0, kv1, out0, out1, h2, c, qc0, qc1, m0, m1, o0, o1):
    scaled, _ = standardize(h1[...])
    c[...] = (scaled * gains[1:2] + biases[1:2]).astype(LOW)
    images = memory.shape[0] // span
    pair_rows = h1.shape[0] // images
    for weight, query, kv, saved in ((q0, qc0, kv0, m0), (q1, qc1, kv1, m1)):
        query[...] = nn(c[...], weight[...]).astype(LOW)
        for j in range(2):
            saved[j] = nn(memory[...], kv[j]).astype(LOW)
    for query, saved, mixed in ((qc0, m0, o0), (qc1, m1, o1)):

        @pl.loop(0, images)
        def _(step):
            rows = pl.ds(pl.multiple_of(step * pair_rows, pair_rows), pair_rows)
            keys = pl.ds(pl.multiple_of(step * span, span), span)
            for lane in range(0, saved.shape[2], PAIR):
                lanes = slice(lane, lane + PAIR)
                mixed[rows, lanes] = attend(
                    query[rows, lanes], saved[0, keys, lanes], saved[1, keys, lanes], None
                )

    h2[...] = h1[...] + (nn(o0[...], out0[...]) + nn(o1[...], out1[...]))


def mlp(
    chunk, h2, cot, gains, biases, up0, up1, down0, down1,
    result, dh2, g0, g1, gain_grad, bias_grad, acc, back, low_ref, parts, sems,
):
    width = h2.shape[1]
    scaled, inverse = standardize(h2[...])
    low_ref[...] = (scaled * gains[2:3] + biases[2:3]).astype(LOW)
    acc[...] = h2[...]
    back[...] = jnp.zeros_like(back)
    hidden = up0.shape[1]
    turned = low_ref[...].T
    store = Stores(sems)
    for half, (up, down, grads) in enumerate(((up0, down0, g0), (up1, down1, g1))):
        for start in range(0, hidden, chunk):
            cols = slice(start, start + chunk)
            u = nn(low_ref[...], up[:, cols])
            below = 0.5 + 0.5 * lax.erf(u * ROOT_HALF)
            z = (u * below).astype(LOW)
            acc[...] += nn(z, down[cols, :])
            dz = nt(cot[...], down[cols, :])
            slope = below + u * (PDF_SCALE * jnp.exp(-0.5 * u * u))
            du = (dz * slope).astype(LOW)
            back[...] += nt(du, up[:, cols])
            down_rows = slice(hidden // chunk * width + start, hidden // chunk * width + start + chunk)
            parts[half, down_rows, :] = tn(z, cot[...]).astype(LOW)
            store(parts.at[half, down_rows], grads.at[down_rows])
            up_rows = slice(start // chunk * width, start // chunk * width + width)
            parts[half, up_rows, :] = nn(turned, du).astype(LOW)
            store(parts.at[half, up_rows], grads.at[up_rows])
    result[...] = acc[...].astype(LOW)
    grad = back[...]
    scaled, inverse = standardize(h2[...])
    gain_grad[...] = column_sum(grad * scaled)
    bias_grad[...] = column_sum(grad)
    dh2[...] = cot[...].astype(F32) + standardize_back(grad, scaled, inverse, gains[2:3])
    store.wait()


def cross_back(
    span, dh2, h1, memory, gains, c, q0, q1, kv0, kv1, out0, out1, qc0, qc1, m0, m1, o0, o1,
    dh1, g0, g1, memory_grad, gain_grad, bias_grad, low, dmix, dq, dkv, back, mem_acc, kv_part, query_part, out_part, sems,
):
    store = Stores(sems)
    low[...] = dh2[...].astype(LOW)
    images = memory.shape[0] // span
    pair_rows = h1.shape[0] // images
    local = q0.shape[1]
    width = h1.shape[1]
    for half, (query, kv, out, qc, saved, mixed, grads) in enumerate(
        ((q0, kv0, out0, qc0, m0, o0, g0), (q1, kv1, out1, qc1, m1, o1, g1))
    ):
        out_part[half] = tn(mixed[...], low[...]).astype(LOW)
        store(out_part.at[half], grads.at[3 * width + local : 4 * width])
        dmix[...] = nt(low[...], out[...]).astype(LOW)

        @pl.loop(0, images)
        def _(step):
            rows = pl.ds(pl.multiple_of(step * pair_rows, pair_rows), pair_rows)
            keys = pl.ds(pl.multiple_of(step * span, span), span)
            for lane in range(0, local, PAIR):
                lanes = slice(lane, lane + PAIR)
                a, b, d = attend_back(
                    qc[rows, lanes], saved[0, keys, lanes], saved[1, keys, lanes], dmix[rows, lanes], None
                )
                dq[rows, lanes] = a
                dkv[0, keys, lanes] = b
                dkv[1, keys, lanes] = d

        query_part[half] = tn(c[...], dq[...]).astype(LOW)
        store(query_part.at[half], grads.at[width : 2 * width, local:])
        kv_part[half, :, :local] = tn(memory[...], dkv[0]).astype(LOW)
        kv_part[half, :, local:] = tn(memory[...], dkv[1]).astype(LOW)
        store(kv_part.at[half], grads.at[2 * width : 3 * width])
        more = nt(dq[...], query[...])
        more_memory = nt(dkv[0], kv[0]) + nt(dkv[1], kv[1])
        if half == 0:
            back[...] = more
            mem_acc[...] = more_memory
        else:
            grad = back[...] + more
            total = (mem_acc[...] + more_memory).astype(LOW)
            memory_grad[0] = total[:, :local]
            memory_grad[1] = total[:, local:]
            scaled, inverse = standardize(h1[...])
            gain_grad[...] = column_sum(grad * scaled)
            bias_grad[...] = column_sum(grad)
            dh1[...] = dh2[...] + standardize_back(grad, scaled, inverse, gains[1:2])
    store.wait()


def self_back(
    length, dh1, x, gains, biases, qkv0, qkv1, out0, out1, s0, s1, o0, o1, old0, old1,
    result, g0, g1, gain_grad, bias_grad, low, a_ref, dmix, dqkv, back, pair_part, value_part, out_part, sems,
):
    store = Stores(sems)
    low[...] = dh1[...].astype(LOW)
    scaled, inverse = standardize(x[...].astype(F32))
    a_ref[...] = (scaled * gains[0:1] + biases[0:1]).astype(LOW)
    pair_rows = 2 * length
    groups = x.shape[0] // pair_rows
    local = o0.shape[1]
    width = x.shape[1]
    turned = a_ref[...].T
    for half, (qkv, out, saved, mixed, grads) in enumerate(
        ((qkv0, out0, s0, o0, g0), (qkv1, out1, s1, o1, g1))
    ):
        out_part[half] = tn(mixed[...], low[...]).astype(LOW)
        store(out_part.at[half], grads.at[3 * width : 3 * width + local])
        dmix[...] = nt(low[...], out[...]).astype(LOW)

        @pl.loop(0, groups)
        def _(step):
            rows = pl.ds(pl.multiple_of(step * pair_rows, pair_rows), pair_rows)
            allowed = caption_mask(pair_rows, length)
            for lane in range(0, local, PAIR):
                lanes = slice(lane, lane + PAIR)
                a, b, d = attend_back(
                    saved[0, rows, lanes], saved[1, rows, lanes], saved[2, rows, lanes], dmix[rows, lanes], allowed
                )
                dqkv[0, rows, lanes] = a
                dqkv[1, rows, lanes] = b
                dqkv[2, rows, lanes] = d

        pair_part[half, :, :local] = nn(turned, dqkv[0]).astype(LOW)
        pair_part[half, :, local:] = nn(turned, dqkv[1]).astype(LOW)
        store(pair_part.at[half], grads.at[0:width])
        value_part[half] = nn(turned, dqkv[2]).astype(LOW)
        store(value_part.at[half], grads.at[width : 2 * width, :local])
        more = nt(dqkv[0], qkv[0]) + nt(dqkv[1], qkv[1]) + nt(dqkv[2], qkv[2])
        if half == 0:
            back[...] = more
        else:
            grad = back[...] + more
            scaled, inverse = standardize(x[...].astype(F32))
            gain_grad[...] = column_sum(grad * scaled)
            bias_grad[...] = column_sum(grad)
            result[...] = (dh1[...] + standardize_back(grad, scaled, inverse, gains[0:1])).astype(LOW)
    store.wait()


def partner(axis):
    dp = lax.axis_index("dp")
    side = lax.axis_index("tensor")
    if axis == "y":
        return dp, 1 - side
    if axis == "core":
        return dp + 1 - 2 * (dp % 2), side
    return dp + 2 - 4 * ((dp // 2) % 2), side


def greet(devices):
    barrier = pltpu.get_barrier_semaphore()
    for device in devices:
        pl.semaphore_signal(barrier, inc=1, device_id=device, device_id_type=MESH)
    pl.semaphore_wait(barrier, len(devices))


def remote(source, target, send, recv, device):
    return pltpu.make_async_remote_copy(
        src_ref=source, dst_ref=target, send_sem=send, recv_sem=recv, device_id=device, device_id_type=MESH
    )


def fetch_weights(count, *refs):
    mine, theirs = refs[:count], refs[count : 2 * count]
    sent, got = refs[2 * count :]
    y, x, core = partner("y"), partner("x"), partner("core")
    dp = lax.axis_index("dp")
    here = dp % 4
    there = here + 2 - 4 * (here // 2)
    greet((y, x, core))

    def piece(ref, number):
        size = ref.shape[0] // 4
        return ref.at[pl.ds(pl.multiple_of(number * size, size), size)]

    def move(k, lane, number, device, source=None):
        spot = piece(theirs[k], number)
        return remote(spot if source is None else source, spot, sent.at[lane, k], got.at[lane, k], device)

    first = [move(k, 0, here, y, piece(mine[k], here)) for k in range(count)]
    for copy in first:
        copy.start()
    later = []
    for k in range(count):
        first[k].wait_recv()
        for lane, device in ((1, x), (2, core)):
            copy = move(k, lane, here, device)
            copy.start()
            later.append(copy)
    last = []
    for k in range(count):
        later[2 * k].wait_recv()
        copy = move(k, 3, there, core)
        copy.start()
        last.append(copy)
    for k in range(count):
        later[2 * k + 1].wait_recv()
        last[k].wait_recv()
    for copy in first + later + last:
        copy.wait_send()


def reduce_grads(chips, *refs):
    (m0, m1, a0, a1, out_half, in_half, mem_half, m_sum, a_sum, out_all, in_all, mem_all) = refs[:12]
    (own, other, core_own, core_other, from_y, ring, local_sem, core_sent, core_got, y_sent, y_got,
     ring_sent, ring_got, gather_sent, gather_got, back_sent, back_got, final_sem, act_sem, act_sent, act_got) = refs[12:]
    dp = lax.axis_index("dp")
    side = lax.axis_index("tensor")
    core = dp % 2
    line = dp // 4
    lane = (dp // 2) % 2
    long = chips // 2
    place = line + lane * (chips - 1 - 2 * line)

    def at(position):
        position = (position + chips) % chips
        x = position // long
        z = position + x * (chips - 1 - 2 * position)
        return 4 * z + 2 * x + core, side

    y, mate = partner("y"), partner("core")
    toward = (at(place + 1), at(place - 1))
    greet((y, mate, *toward))
    rows = own.shape[3]
    quarter = chips * rows

    def spot(ref, which, direction, number):
        base = (which * 2 + direction) * quarter + number * rows
        return ref.at[pl.ds(pl.multiple_of(base, rows), rows)]

    def number(direction, step):
        return (place + (2 * chips - step if direction == 0 else step)) % chips

    parts = ((m0, m1, m_sum), (a0, a1, a_sum))
    lanes = [(p, d) for p in range(2) for d in range(2)]

    def acts():
        copies = []
        for i, (half, whole) in enumerate(((out_half, out_all), (in_half, in_all))):
            size = half.shape[0]
            target = whole.at[pl.ds(pl.multiple_of(side * size, size), size)]
            copies.append((half, half, target, i))
        size = mem_half.shape[1]
        target = mem_all.at[pl.ds(pl.multiple_of(side * size, size), size)]
        copies.append((mem_half.at[side], mem_half.at[1 - side], target, 2))
        local = [pltpu.make_async_copy(a, t, act_sem.at[i]) for a, _, t, i in copies]
        away = [remote(b, t, act_sent.at[i], act_got.at[i], y) for _, b, t, i in copies]
        return local, away

    def loads(p, d, s):
        k = number(d, s)
        return (
            pltpu.make_async_copy(spot(parts[p][0], core, d, k), own.at[p, d, s], local_sem.at[0, p, d, s]),
            pltpu.make_async_copy(spot(parts[p][1], core, d, k), other.at[p, d, s], local_sem.at[1, p, d, s]),
        )

    def to_mate(p, d, s):
        k = number(d, s)
        return (
            remote(spot(parts[p][0], 1 - core, d, k), core_own.at[p, d, s], core_sent.at[0, p, d, s],
                   core_got.at[0, p, d, s], mate),
            remote(spot(parts[p][1], 1 - core, d, k), core_other.at[p, d, s], core_sent.at[1, p, d, s],
                   core_got.at[1, p, d, s], mate),
        )

    def to_y(p, d, s):
        return remote(other.at[p, d, s], from_y.at[p, d, s], y_sent.at[p, d, s], y_got.at[p, d, s], y)

    def to_next(p, d, s):
        return remote(own.at[p, d, s], ring.at[p, d, s], ring_sent.at[p, d, s], ring_got.at[p, d, s], toward[d])

    def gather(p, d, s):
        k = number(d, s + chips - 1)
        source = own.at[p, d, chips - 1] if isinstance(s, int) and s == 0 else spot(parts[p][2], core, d, k)
        return remote(source, spot(parts[p][2], core, d, k), gather_sent.at[p, d, s], gather_got.at[p, d, s], toward[d])

    def give_back(p, d, s):
        k = number(d, s + chips - 1)
        source = own.at[p, d, chips - 1] if isinstance(s, int) and s == 0 else spot(parts[p][2], core, d, k)
        return remote(source, spot(parts[p][2], core, d, k), back_sent.at[p, d, s], back_got.at[p, d, s], mate)

    @pl.loop(0, chips)
    def _(s):
        for p, d in lanes:
            for copy in (*loads(p, d, s), *to_mate(p, d, s)):
                copy.start()

    def first(s):
        for p, d in lanes:
            for copy in loads(p, d, s):
                copy.wait()
            for copy in to_mate(p, d, s):
                copy.wait_recv()
            other[p, d, s] = (other[p, d, s].astype(F32) + core_other[p, d, s].astype(F32)).astype(LOW)
            to_y(p, d, s).start()

    def second(s, start):
        for p, d in lanes:
            to_y(p, d, s).wait_recv()
            total = own[p, d, s].astype(F32) + core_own[p, d, s].astype(F32) + from_y[p, d, s].astype(F32)
            if not start:
                to_next(p, d, s - 1).wait_recv()
                total = total + ring[p, d, s - 1].astype(F32)
            own[p, d, s] = total.astype(LOW)

    first(0)
    first(1)
    second(0, True)
    for p, d in lanes:
        to_next(p, d, 0).start()

    @pl.loop(1, chips - 1)
    def _(s):
        first(s + 1)
        second(s, False)
        for p, d in lanes:
            to_next(p, d, s).start()

    local, away = acts()
    for copy in local + away:
        copy.start()
    second(chips - 1, False)
    finals = []
    for p, d in lanes:
        k = number(d, chips - 1)
        copy = pltpu.make_async_copy(own.at[p, d, chips - 1], spot(parts[p][2], core, d, k), final_sem.at[p, d])
        copy.start()
        finals.append(copy)
        gather(p, d, 0).start()
        give_back(p, d, 0).start()

    @pl.loop(1, chips - 1)
    def _(s):
        for p, d in lanes:
            gather(p, d, s - 1).wait_recv()
            gather(p, d, s).start()
            give_back(p, d, s).start()

    for p, d in lanes:
        gather(p, d, chips - 2).wait_recv()
        give_back(p, d, chips - 1).start()

    for copy in finals + local:
        copy.wait()
    for copy in away:
        copy.wait()

    @pl.loop(0, chips)
    def _(s):
        for p, d in lanes:
            for copy in to_mate(p, d, s):
                copy.wait_send()
            to_y(p, d, s).wait_send()
            give_back(p, d, s).wait()

    @pl.loop(0, chips - 1)
    def _(s):
        for p, d in lanes:
            to_next(p, d, s).wait_send()
            gather(p, d, s).wait_send()


def take_rows(order_ref, a_ref, b_ref, a_out, b_out):
    a_out[...] = a_ref[...]
    b_out[...] = b_ref[...]


def take_captions(order, length, first, second):
    width = first.shape[1]
    count = order.shape[0]
    source = pl.BlockSpec((length, width), lambda i, order_ref: (order_ref[i], 0))
    target = pl.BlockSpec((length, width), lambda i, order_ref: (i, 0))
    shape = jax.ShapeDtypeStruct((count * length, width), first.dtype)
    return pl.pallas_call(
        take_rows,
        grid_spec=pltpu.PrefetchScalarGridSpec(
            num_scalar_prefetch=1, grid=(count,), in_specs=[source, source], out_specs=[target, target]
        ),
        out_shape=[shape, shape],
        name="take_captions",
    )(order, first, second)


def put_captions(order, length, first, second):
    width = first.shape[1]
    count = order.shape[0]
    source = pl.BlockSpec((length, width), lambda i, order_ref: (i, 0))
    target = pl.BlockSpec((length, width), lambda i, order_ref: (order_ref[i], 0))
    shape = jax.ShapeDtypeStruct((count * length, width), first.dtype)
    return pl.pallas_call(
        take_rows,
        grid_spec=pltpu.PrefetchScalarGridSpec(
            num_scalar_prefetch=1, grid=(count,), in_specs=[source, source], out_specs=[target, target]
        ),
        out_shape=[shape, shape],
        name="put_captions",
    )(order, first, second)


def shape(dims, kind=LOW):
    return jax.ShapeDtypeStruct(dims, kind)


def call(body, name, args, outs, scratch, specs=None, out_specs=None, **params):
    return pl.pallas_call(
        body,
        out_shape=outs,
        in_specs=specs if specs is not None else [VMEM] * len(args),
        out_specs=out_specs if out_specs is not None else [VMEM] * len(outs),
        scratch_shapes=scratch,
        input_output_aliases=params.pop("aliases", {}),
        compiler_params=pltpu.CompilerParams(vmem_limit_bytes=VMEM_LIMIT, **params),
        name=name,
    )(*args)


def shards(
    chips, tokens, memory, groups, gains, biases, self_qkv, self_out, cross_query, cross_kv,
    cross_out, mlp_up, mlp_down, cotangent,
):
    captions = groups.shape[0]
    length = tokens.shape[0] // captions
    width = tokens.shape[1]
    images, span = memory.shape[:2]
    local = self_qkv.shape[2]
    hidden = mlp_up.shape[1]
    side = lax.axis_index("tensor")
    some = captions // 2 * length
    rows = images // 2 * span

    picked = groups - lax.axis_index("dp") * images
    same = picked[:, None] == picked[None, :]
    number = lax.broadcasted_iota(jnp.int32, (captions, captions), 0)
    other = lax.broadcasted_iota(jnp.int32, (captions, captions), 1)
    rank = 2 * picked + jnp.sum((same & (other < number)).astype(jnp.int32), axis=1)
    order = jnp.sum(jnp.where(rank[None, :] == number, other, 0), axis=1)
    mine = lax.dynamic_slice_in_dim(order, side * (captions // 2), captions // 2)
    x, cot = take_captions(mine, length, tokens, cotangent)
    some_memory = lax.dynamic_slice_in_dim(memory, side * (images // 2), images // 2).reshape(rows, width)

    weights = [
        self_qkv.reshape(3 * width, local), self_out, cross_kv.reshape(2 * width, local), cross_query,
        cross_out, mlp_up, mlp_down,
    ]
    count = len(weights)
    fetched = call(
        functools.partial(fetch_weights, count), "fetch_weights", weights, [shape(w.shape) for w in weights],
        [pltpu.SemaphoreType.DMA((4, count))] * 2, [ANY] * count, [ANY] * count,
        collective_id=0, has_side_effects=True,
    )
    qkv = (self_qkv, fetched[0].reshape(3, width, local))
    out = (self_out, fetched[1])
    kv = (cross_kv, fetched[2].reshape(2, width, local))
    query = (cross_query, fetched[3])
    mix = (cross_out, fetched[4])
    up = (mlp_up, fetched[5])
    down = (mlp_down, fetched[6])

    h1, s0, s1, o0, o1 = call(
        functools.partial(self_forward, length), "self_forward", (x, gains, biases, *qkv, *out),
        [shape((some, width), F32)] + [shape((3, some, local))] * 2 + [shape((some, local))] * 2, [],
    )
    h2, c, qc0, qc1, kv0, kv1, oc0, oc1 = call(
        functools.partial(cross_forward, span), "cross_forward",
        (h1, some_memory, gains, biases, *query, *kv, *mix),
        [shape((some, width), F32), shape((some, width))] + [shape((some, local))] * 2
        + [shape((2, rows, local))] * 2 + [shape((some, local))] * 2, [],
    )
    part = hidden * 2
    row = shape((1, width), F32)
    chunk = min(hidden, width)
    y_half, dh2, gm0, gm1, gain2, bias2 = call(
        functools.partial(mlp, chunk), "mlp", (h2, cot, gains, biases, *up, *down),
        [shape((some, width)), shape((some, width), F32), shape((part, width)), shape((part, width)), row, row],
        [pltpu.VMEM((some, width), F32), pltpu.VMEM((some, width), F32), pltpu.VMEM((some, width), LOW),
         pltpu.VMEM((2, part, width), LOW), pltpu.SemaphoreType.DMA((4 * hidden // chunk,))],
        out_specs=[VMEM, VMEM, ANY, ANY, VMEM, VMEM],
    )
    attn_rows = 4 * width
    dh1, ga0, ga1, mem_half, gain1, bias1 = call(
        functools.partial(cross_back, span), "cross_back",
        (dh2, h1, some_memory, gains, c, *query, *kv, *mix, qc0, qc1, kv0, kv1, oc0, oc1),
        [shape((some, width), F32), shape((attn_rows, width)), shape((attn_rows, width)), shape((2, rows, local)), row, row],
        [pltpu.VMEM((some, width), LOW), pltpu.VMEM((some, local), LOW), pltpu.VMEM((some, local), LOW),
         pltpu.VMEM((2, rows, local), LOW), pltpu.VMEM((some, width), F32), pltpu.VMEM((rows, width), F32),
         pltpu.VMEM((2, width, width), LOW), pltpu.VMEM((2, width, local), LOW), pltpu.VMEM((2, local, width), LOW),
         pltpu.SemaphoreType.DMA((6,))],
        out_specs=[VMEM, ANY, ANY, VMEM, VMEM, VMEM],
    )
    x_half, ga0, ga1, gain0, bias0 = call(
        functools.partial(self_back, length), "self_back",
        (dh1, x, gains, biases, *qkv, *out, s0, s1, o0, o1, ga0, ga1),
        [shape((some, width)), shape((attn_rows, width)), shape((attn_rows, width)), row, row],
        [pltpu.VMEM((some, width), LOW), pltpu.VMEM((some, width), LOW), pltpu.VMEM((some, local), LOW),
         pltpu.VMEM((3, some, local), LOW), pltpu.VMEM((some, width), F32),
         pltpu.VMEM((2, width, width), LOW), pltpu.VMEM((2, width, local), LOW), pltpu.VMEM((2, local, width), LOW),
         pltpu.SemaphoreType.DMA((6,))],
        specs=[VMEM] * 12 + [ANY] * 2, out_specs=[VMEM, ANY, ANY, VMEM, VMEM], aliases={12: 1, 13: 2},
    )
    small = lax.psum(jnp.concatenate([gain0, gain1, gain2, bias0, bias1, bias2], axis=0), ("dp", "tensor"))

    block = part // (4 * chips)
    cube = pltpu.VMEM((2, 2, chips, block, width), LOW)
    dma = pltpu.SemaphoreType.DMA
    full = dma((2, 2, chips))
    m_sum, a_sum, y_all, x_all, mem_all = call(
        functools.partial(reduce_grads, chips), "reduce_grads", (gm0, gm1, ga0, ga1, y_half, x_half, mem_half),
        [shape((part, width)), shape((attn_rows, width)), shape((2 * some, width)), shape((2 * some, width)),
         shape((2 * rows, local))],
        [cube] * 5 + [pltpu.VMEM((2, 2, chips - 1, block, width), LOW)]
        + [dma((2, 2, 2, chips))] * 3 + [full] * 8 + [dma((2, 2))] + [dma((3,))] * 3,
        [ANY] * 7, [ANY] * 5, collective_id=1, has_side_effects=True,
    )
    output, input_grad = put_captions(order, length, y_all, x_all)
    memory_grad = mem_all.reshape(images, span, local)
    wide_m = m_sum.astype(F32)
    blocks = hidden // chunk
    up_grad = jnp.concatenate([wide_m[i * width : (i + 1) * width] for i in range(blocks)], axis=1)
    down_grad = wide_m[blocks * width :]
    wide_a = a_sum.astype(F32)
    qkv_grad = jnp.stack([wide_a[:width, :local], wide_a[:width, local:], wide_a[width : 2 * width, :local]])
    query_grad = wide_a[width : 2 * width, local:]
    kv_grad = jnp.stack([wide_a[2 * width : 3 * width, :local], wide_a[2 * width : 3 * width, local:]])
    out_grad = wide_a[3 * width : 3 * width + local]
    mix_grad = wide_a[3 * width + local :]
    return (
        output, input_grad, memory_grad, small[:3], small[3:], qkv_grad, out_grad, query_grad, kv_grad,
        mix_grad, up_grad, down_grad,
    )


def solution(mesh):
    rows = P("dp", None)
    columns = P(None, "tensor")
    stacked = P(None, None, "tensor")
    halves = P("tensor", None)
    return jax.shard_map(
        functools.partial(shards, mesh.shape["dp"] // 2),
        mesh=mesh,
        in_specs=(rows, P("dp", None, None), P("dp"), P(), P(), stacked, halves, columns, stacked, halves, columns, halves, rows),
        out_specs=(
            rows, rows, P("dp", None, "tensor"), P(), P(), stacked, halves, columns, stacked, halves, columns, halves,
        ),
        check_vma=False,
    )
```

time: 981 us -> 463 us (0.47)
  waiting for transfers between devices: 519 us -> 0 us
  Pallas kernels: 0 us -> 393 us
  local copies, waits for them, and re-layouts: 164 us -> 12.5 us
  matrix products: 141 us -> 0 us
  other arithmetic: 55.3 us -> 9.19 us
  blocking collectives: 65 us -> 39.7 us
  between operations: 15.6 us -> 1.29 us
  starting transfers between devices: 11.5 us -> 0 us
    psum x6 -> x0, waiting for transfers between devices: 518 us -> none  [the longest x1 265 us: shards(): lax.psum((self_qkv_grad, self_out_grad, gain_one, bias_one), 'dp')]
    pallas_call x0 -> x9, Pallas kernels: none -> 393 us  [the longest x7 376 us: call(): pl.pallas_call(body, out_shape=outs, in_specs=specs if specs is not None...]
    dot_general x34 -> x0, matrix products: 141 us -> none  [the longest x5 27.8 us: back_product(): jnp.einsum('td,fd->tf', grad_side, weight, preferred_element_type=jnp.flo...]
    unnamed x155 -> x27, local copies, waits for them, and re-layouts: 57.6 us -> 1.63 us
    another operation x18 -> x1, local copies, waits for them, and re-layouts: 48.4 us -> 0.38 us  [shards(): jnp.stack([wide_a[2 * width:3 * width, :local], wide_a[2 * width:3 * widt...]
    psum x1, blocking collectives: 65 us -> 39.7 us  [shards(): lax.psum(jnp.concatenate([gain0, gain1, gain2, bias0, bias1, bias2], axis...]
    reduce_sum x11 -> x2, other arithmetic: 24.8 us -> 0.3 us  [the longest x1 0.18 us: shards(): jnp.sum((same & (other < number)).astype(jnp.int32), axis=1)]
    reshape x7 -> x0, local copies, waits for them, and re-layouts: 22.1 us -> none  [the longest x2 6.03 us: shards(): back_product(cross_branch, cross_out).astype(jnp.bfloat16)]
  transfers between devices with their start and end apart: 7 -> 0, of which waited for: 6 -> 0; matrix products, arithmetic and copies ran while one was open for 19% -> 0% of each run, Pallas kernels for 0% -> 0%
where the time goes in v1:
time: 463 us; the launch traced here: 456 us
  Pallas kernels  393 us (85%)
  blocking collectives  39.7 us (9%)
  local copies, waits for them, and re-layouts  12.5 us (3%)
  other arithmetic  9.19 us (2%)
    pallas_call x7, Pallas kernels, call(): pl.pallas_call(body, out_shape=outs, in_specs=specs if specs is not None...  376 us
    psum x1, blocking collectives, shards(): lax.psum(jnp.concatenate([gain0, gain1, gain2, bias0, bias1, bias2], axis...  39.7 us
    pallas_call x1, Pallas kernels, put_captions(): pl.pallas_call(take_rows, grid_spec=pltpu.PrefetchScalarGridSpec(num_scal...  10.7 us

profile of v1, /device:TPU:0, one launch (start us, length us, event | category | flops | bytes accessed | tf_op | source)
XLA Modules:
  0.0 455.7 jit_solution(16296992423653314363)
XLA Ops:
  0.6 0.0 copy-start
  0.7 0.8 broadcast_subtract_fusion
  1.5 0.2 convert_reduce_fusion
  1.7 0.7 multiply_add_fusion
  2.3 0.1 select_reduce_fusion.order_ref
  2.4 0.6 dynamic_slice.6.order_ref
  3.0 1.2 constant_dynamic-slice_fusion
  4.3 6.1 %take_captions.1 = (bf16[512,768]{1,0:T(8,128)(2,1)}, bf16[512,768]{1,0:T(8,128)(2,1)}) custom-call(s32[8]{0:T(128)} %dynamic_slice.6.order_ref, bf16[1024,768]{1,0:T(8,128)(2,1)} %a_ref.1, bf16[1024,768]{1,0:T(8,128)(2,1)} %b_ref.1), custom_call_target="tpu_custom_call" | custom-call | tf_op jit(solution)/shard_map/take_captions/pallas_call | solution.py:545
  10.4 72.4 %fetch_weights.1 = (bf16[2304,384]{1,0:T(8,128)(2,1)}, bf16[384,768]{1,0:T(8,128)(2,1)}, bf16[1536,384]{1,0:T(8,128)(2,1)}, bf16[768,384]{1,0:T(8,128)(2,1)}, bf...) custom-call(bf16[2304,384]{1,0:T(8,128)(2,1)} %bitcast.18, bf16[384,768]{1,0:T(8,128)(2,1)} %out0.7, ...), custom_call_target="tpu_custom_call" | custom-call | tf_op jit(solution)/shard_map/fetch_weights/pallas_call | solution.py:576
  82.8 23.9 %self_forward.1 = (f32[512,768]{1,0:T(8,128)}, bf16[3,512,384]{2,1,0:T(8,128)(2,1)}, bf16[3,512,384]{2,1,0:T(8,128)(2,1)}, bf16[512,384]{1,0:T(8,128)(2,1)}, bf16[512,384]{1,0:T(8,128)(2,1)}) custom-call(bf16[512,768]{1,0:T(8,128)(2,1)} %get-tuple-element.58.x, f32[3,768]{1,0:T(4,128)} %gains.9, f32[3,768]{1,0:T(4,128)} %biases.7, ...), custom_call_target="tpu_custom_call" | custom-call | tf_op jit(solution)/shard_map/self_forward/pallas_call | solution.py:576
  106.8 18.3 %cross_forward.1 = (f32[512,768]{1,0:T(8,128)}, bf16[512,768]{1,0:T(8,128)(2,1)}, bf16[512,384]{1,0:T(8,128)(2,1)}, bf16[512,384]{1,0:T(8,128)(2,1)}, bf16[2,102...) custom-call(f32[512,768]{1,0:T(8,128)} %get-tuple-element.61.h1, ...), custom_call_target="tpu_custom_call" | custom-call | tf_op jit(solution)/shard_map/cross_forward/pallas_call | solution.py:576
  125.1 23.0 %mlp.1 = (bf16[512,768]{1,0:T(8,128)(2,1)}, f32[512,768]{1,0:T(8,128)}, bf16[3072,768]{1,0:T(8,128)(2,1)}, bf16[3072,768]{1,0:T(8,128)(2,1)}, f32[1,768]{1,0:T(1,128)}, /*index=5*/f32[1,768]{1,0:T(1,128)}) custom-call(f32[512,768]{1,0:T(8,128)} %get-tuple-element.65.h2, bf16[512,768]{1,0:T(8,128)(2,1)} %get-tuple-element.66.cot, f32[3,768]{1,0:T(4,128)} %gains.9, ...), custom_call_target="tpu_custom_call" | custom-call | tf_op jit(solution)/shard_map/mlp/pallas_call | solution.py:576
  148.1 36.9 %cross_back.1 = (f32[512,768]{1,0:T(8,128)}, bf16[3072,768]{1,0:T(8,128)(2,1)}, bf16[3072,768]{1,0:T(8,128)(2,1)}, bf16[2,1024,384]{2,1,0:T(8,128)(2,1)}, f32[1,768]{1,0:T(1,128)}, /*index=5*/f32[1,768]{1,0:T(1,128)}) custom-call(f32[512,768]{1,0:T(8,128)} %get-tuple-element.71.dh2, f32[512,768]{1,0:T(8,128)} %get-tuple-element.61.h1, ...), custom_call_target="tpu_custom_call" | custom-call | tf_op jit(solution)/shard_map/cross_back/pallas_call | solution.py:576
  185.0 30.8 %self_back.1 = (bf16[512,768]{1,0:T(8,128)(2,1)}, bf16[3072,768]{1,0:T(8,128)(2,1)}, bf16[3072,768]{1,0:T(8,128)(2,1)}, f32[1,768]{1,0:T(1,128)}, f32[1,768]{1,0:T(1,128)}) custom-call(f32[512,768]{1,0:T(8,128)} %get-tuple-element.79.dh1, bf16[512,768]{1,0:T(8,128)(2,1)} %get-tuple-element.58.x, ...), custom_call_target="tpu_custom_call", output_to_operand_aliasing={{1}: (12, {}), {2}: (13, {})} | custom-call | tf_op jit(solution)/shard_map/self_back/pallas_call | solution.py:576
  215.7 170.9 %reduce_grads.1 = (bf16[3072,768]{1,0:T(8,128)(2,1)}, bf16[3072,768]{1,0:T(8,128)(2,1)}, bf16[1024,768]{1,0:T(8,128)(2,1)}, bf16[1024,768]{1,0:T(8,128)(2,1)}, bf16[2048,384]{1,0:T(8,128)(2,1)}) custom-call(bf16[3072,768]{1,0:T(8,128)(2,1)} %get-tuple-element.69.refs_0_, bf16[3072,768]{1,0:T(8,128)(2,1)} %get-tuple-element.70.refs_1_, ...), custom_call_target="tpu_custom_call" | custom-call | tf_op jit(solution)/shard_map/reduce_grads/pallas_call | solution.py:576
  386.7 0.0 copy-start.4
  386.7 0.0 copy-start.5
  386.7 10.7 %put_captions.1 = (bf16[1024,768]{1,0:T(8,128)(2,1)}, bf16[1024,768]{1,0:T(8,128)(2,1)}) custom-call(s32[16]{0:T(128)} %copy-done.10, bf16[1024,768]{1,0:T(8,128)(2,1)} %get-tuple-element.91.a_ref, bf16[1024,768]{1,0:T(8,128)(2,1)} %get-tuple-element.92.b_ref), custom_call_target="tpu_custom_call" | custom-call | tf_op jit(solution)/shard_map/put_captions/pallas_call | solution.py:561
  397.5 39.7 %psum.7 = f32[6,768]{1,0:T(8,128)S(1)} all-reduce(f32[6,768]{1,0:T(8,128)S(1)} %concatenate.6), channel_id=1, replica_groups=mesh['dp'=16,'tensor'=2] {'dp','tensor'}, use_global_device_ids=true, to_apply=%region_2.3 | all-reduce | flops 4608 | bytes 36864 | tf_op jit(solution)/shard_map/psum | solution.py:671
  437.2 0.6 fusion.3
  437.8 2.2 slice.58
  440.0 3.0 fusion.2
  442.9 0.2 copy-done.2
  443.1 0.7 convert_element_type.10
  443.9 0.4 slice_bitcast_fusion.1
  444.3 1.6 pad_maximum_fusion.2
  445.8 2.0 pad_maximum_fusion.1
  447.9 0.2 slice-done.1
  448.1 2.5 slice.64
  450.6 0.4 fusion.1
  451.0 3.1 pad_maximum_fusion
  454.1 1.1 copy.30
  (23 shorter events, 0.1 us)
Async XLA Ops:
  0.6 2.4 copy-start
  2.4 8.0 %copy-start.10 = (s32[16]{0:T(128)}, s32[16]{0:T(128)S(1)}, u32[]{:S(2)}) copy-start(s32[16]{0:T(128)S(1)} %select_reduce_fusion.order_ref) | copy-start | bytes 196
  386.7 10.8 %copy-start.4 = (f32[1,768]{1,0:T(1,128)S(1)}, f32[1,768]{1,0:T(1,128)}, u32[]{:S(2)}) copy-start(f32[1,768]{1,0:T(1,128)} %get-tuple-element.98) | copy-start | bytes 9220
  386.7 10.7 %copy-start.5 = (f32[1,768]{1,0:T(1,128)S(1)}, f32[1,768]{1,0:T(1,128)}, u32[]{:S(2)}) copy-start(f32[1,768]{1,0:T(1,128)} %get-tuple-element.101) | copy-start | bytes 9220
  386.7 10.7 %copy-start.6 = (f32[1,768]{1,0:T(1,128)S(1)}, f32[1,768]{1,0:T(1,128)}, u32[]{:S(2)}) copy-start(f32[1,768]{1,0:T(1,128)} %get-tuple-element.97) | copy-start | bytes 9220
  386.7 10.7 %copy-start.7 = (f32[1,768]{1,0:T(1,128)S(1)}, f32[1,768]{1,0:T(1,128)}, u32[]{:S(2)}) copy-start(f32[1,768]{1,0:T(1,128)} %get-tuple-element.100) | copy-start | bytes 9220
  386.7 10.7 %copy-start.8 = (f32[1,768]{1,0:T(1,128)S(1)}, f32[1,768]{1,0:T(1,128)}, u32[]{:S(2)}) copy-start(f32[1,768]{1,0:T(1,128)} %get-tuple-element.96) | copy-start | bytes 9220
  386.7 10.7 %copy-start.9 = (f32[1,768]{1,0:T(1,128)S(1)}, f32[1,768]{1,0:T(1,128)}, u32[]{:S(2)}) copy-start(f32[1,768]{1,0:T(1,128)} %get-tuple-element.99) | copy-start | bytes 9220
  440.0 3.2 copy-start.2
  443.9 4.0 slice-start
  444.3 3.8 slice-start.1
  451.0 3.1 copy-start.3
  451.0 4.3 copy-start.1
